TPU v7x, 32 devices: a whole 2x2x4 slice. The times are simulated.
32 devices in a mesh: row: 8 (over z, core), col: 2 (over y), head: 2 (over x).
Axes of the slice: x: 2, y: 2, z: 4, core: 2. Of those that a mesh axis runs over, the one named last changes fastest.
Arguments:
- x_lo: float32 [6, 32, 64, 4], P('col', 'row', 'head'), may hold values from -32 to 32
- noise: float32 [6, 32, 64, 16], P('col', 'row'), may hold values from -6 to 6
- t_index: int32 [6], P('col'), may hold values from 0 to 999
- labels: int32 [6], P('col'), may hold values from 0 to 1000
- stale_kv: bfloat16 [2, 6, 16, 32, 1152], P(None, 'col', 'row', None, 'head'), may hold values from -6 to 6
- embed_w: float32 [16, 1152], replicated, may hold values from -1.5 to 1.5
- t_w1: bfloat16 [256, 1152], replicated, may hold values from -0.375 to 0.375
- t_w2: bfloat16 [1152, 1152], P(None, 'row'), may hold values from -0.1875 to 0.1875
- class_table: bfloat16 [1001, 1152], P(None, 'row'), may hold values from -6 to 6
- ada_w: bfloat16 [1152, 6912], P('row'), may hold values from -0.1875 to 0.1875
- qkv_w: bfloat16 [1152, 3, 1152], P(None, None, 'head'), may hold values from -0.1875 to 0.1875
- out_w: bfloat16 [1152, 1152], P('head'), may hold values from -0.1875 to 0.1875
- fc1_w: bfloat16 [1152, 4608], P(None, ('col', 'head')), may hold values from -0.1875 to 0.1875
- fc2_w: bfloat16 [1152, 4608], P(None, ('col', 'head')), may hold values from -0.09375 to 0.09375
Outputs:
- tokens_out: bfloat16 [6, 32, 64, 1152], P('col', 'row', 'head')
All inputs are finite; a program needn't handle non-finite values.
Results may differ from a plain program's by a relative error of at most 0.025.
Values may be sent and summed in bfloat16 or wider, within the bound.
A program may use at most 128 MiB of HBM per device.

v0:
```python
import math
import jax
import jax.numpy as jnp
from jax import lax
from jax.sharding import PartitionSpec as P

HD = 72
TSTEPS = 1000


def padded_2(block, sides, width):
    for axis, dim in sides:
        count = lax.axis_size(axis)
        forward = [(i, i + 1) for i in range(count - 1)]
        backward = [(target, source) for source, target in forward]
        low = lax.ppermute(
            lax.slice_in_dim(block, block.shape[dim] - width, None, axis=dim), axis, forward
        )
        high = lax.ppermute(lax.slice_in_dim(block, 0, width, axis=dim), axis, backward)
        block = jnp.concatenate([low, block, high], axis=dim)
    return block


def upsample_padded(padded):
    upper = padded[:, :-2]
    middle = padded[:, 1:-1]
    lower = padded[:, 2:]
    rows_even = 0.75 * middle + 0.25 * upper
    rows_odd = 0.75 * middle + 0.25 * lower

    def widen(vertical):
        left_side = vertical[:, :, :-2]
        centre = vertical[:, :, 1:-1]
        right_side = vertical[:, :, 2:]
        return jnp.stack(
            [0.75 * centre + 0.25 * left_side, 0.75 * centre + 0.25 * right_side], axis=3
        )

    stacked = jnp.stack([widen(rows_even), widen(rows_odd)], axis=3)
    return stacked.reshape(
        stacked.shape[0], stacked.shape[1], stacked.shape[2], 4 * stacked.shape[-1]
    )


def clamp_edges(padded, axis_dim, at_start, at_end):
    length = padded.shape[axis_dim]
    leading = lax.slice_in_dim(padded, 0, 1, axis=axis_dim)
    second_row = lax.slice_in_dim(padded, 1, 2, axis=axis_dim)
    trailing = lax.slice_in_dim(padded, length - 1, length, axis=axis_dim)
    before_end = lax.slice_in_dim(padded, length - 2, length - 1, axis=axis_dim)
    leading = jnp.where(at_start, second_row, leading)
    trailing = jnp.where(at_end, before_end, trailing)
    return jnp.concatenate(
        [leading, lax.slice_in_dim(padded, 1, length - 1, axis=axis_dim), trailing], axis=axis_dim
    )


def noise_level(t_index):
    step_values = jnp.arange(TSTEPS, dtype=jnp.float32)
    betas = 0.0001 + (0.02 - 0.0001) * step_values / (TSTEPS - 1)
    log_keep = jnp.cumsum(jnp.log(1.0 - betas))
    picked = (jnp.arange(TSTEPS, dtype=jnp.int32)[None, :] == t_index[:, None]).astype(jnp.float32)
    return jnp.exp(jnp.sum(picked * log_keep[None, :], axis=1))


def position_table(row_pos, col_pos, width):
    quarter = width // 4
    omega = 1.0 / 10000.0 ** (jnp.arange(quarter, dtype=jnp.float32) / quarter)
    row_args = row_pos[:, None] * omega[None, :]
    col_args = col_pos[:, None] * omega[None, :]
    row_part = jnp.concatenate([jnp.sin(row_args), jnp.cos(row_args)], axis=1)
    col_part = jnp.concatenate([jnp.sin(col_args), jnp.cos(col_args)], axis=1)
    n_rows = row_pos.shape[0]
    n_cols = col_pos.shape[0]
    return jnp.concatenate(
        [
            jnp.broadcast_to(row_part[:, None, :], (n_rows, n_cols, width // 2)),
            jnp.broadcast_to(col_part[None, :, :], (n_rows, n_cols, width // 2)),
        ],
        axis=2,
    )


def condition(t_index, labels, t_w1, t_w2, class_table):
    half_freq = t_w1.shape[0] // 2
    freqs = jnp.exp(-math.log(10000.0) * jnp.arange(half_freq, dtype=jnp.float32) / half_freq)
    angles = t_index.astype(jnp.float32)[:, None] * freqs[None, :]
    freq_feat = jnp.concatenate([jnp.cos(angles), jnp.sin(angles)], axis=1).astype(jnp.bfloat16)
    t_hidden = jax.nn.silu(jnp.dot(freq_feat, t_w1, preferred_element_type=jnp.float32)).astype(
        jnp.bfloat16
    )
    t_embed = jnp.dot(t_hidden, t_w2, preferred_element_type=jnp.float32)
    onehot = (jnp.arange(class_table.shape[0], dtype=jnp.int32)[None, :] == labels[:, None]).astype(
        jnp.bfloat16
    )
    return t_embed + jnp.dot(onehot, class_table, preferred_element_type=jnp.float32)


def layer_norm(values):
    centre = jnp.mean(values, axis=-1, keepdims=True)
    spread = jnp.mean((values - centre) ** 2, axis=-1, keepdims=True)
    return (values - centre) * lax.rsqrt(spread + 1e-06)


def spread_out(vector):
    return vector[:, None, None, :]


def body(
    x_lo,
    noise,
    t_index,
    labels,
    stale_kv,
    embed_w,
    t_w1,
    t_w2,
    class_table,
    ada_w,
    qkv_w,
    out_w,
    fc1_w,
    fc2_w,
):
    row_index = lax.axis_index("row")
    row_count = lax.axis_size("row")
    head_index = lax.axis_index("head")
    head_count = lax.axis_size("head")
    batch = noise.shape[0]
    tile_rows = noise.shape[1]
    full_cols = noise.shape[2]
    channels = x_lo.shape[3]
    width = embed_w.shape[1]
    abar = noise_level(t_index)
    gathered = lax.all_gather(x_lo, "head", axis=2, tiled=True)
    padded = padded_2(gathered, (("row", 1),), 1)
    padded = clamp_edges(padded, 1, row_index == 0, row_index == row_count - 1)
    padded = jnp.pad(padded, ((0, 0), (0, 0), (1, 1), (0, 0)), mode="edge")
    upsampled = upsample_padded(padded)
    noisy = (
        jnp.sqrt(abar)[:, None, None, None] * upsampled
        + jnp.sqrt(1.0 - abar)[:, None, None, None] * noise
    )
    grouped = noisy.reshape(batch, tile_rows, full_cols, 4, channels)
    total, squares = lax.psum(
        (jnp.sum(grouped, axis=(1, 2, 3)), jnp.sum(grouped * grouped, axis=(1, 2, 3))), "row"
    )
    count = 4.0 * tile_rows * row_count * full_cols
    centre = total / count
    spread = squares / count - centre * centre
    normed = (
        (grouped - centre[:, None, None, None, :])
        * lax.rsqrt(spread + 1e-05)[:, None, None, None, :]
    ).reshape(batch, tile_rows, full_cols, 4 * channels)
    row_pos = (row_index * tile_rows + jnp.arange(tile_rows, dtype=jnp.int32)).astype(jnp.float32)
    col_pos = jnp.arange(full_cols, dtype=jnp.float32)
    pos = position_table(row_pos, col_pos, width)
    tokens = (
        jnp.einsum("bijf,fd->bijd", normed, embed_w, precision=lax.Precision.HIGHEST) + pos[None]
    ).astype(jnp.bfloat16)
    cond_part = condition(t_index, labels, t_w1, t_w2, class_table)
    cond_act = jax.nn.silu(cond_part).astype(jnp.bfloat16)
    modulation = lax.psum(
        jnp.dot(cond_act, ada_w, preferred_element_type=jnp.float32).astype(jnp.bfloat16), "row"
    ).astype(jnp.float32)
    shift1, scale1, gate1, shift2, scale2, gate2 = jnp.split(modulation, 6, axis=1)
    per_image = tile_rows * full_cols
    flat = tokens.astype(jnp.float32)
    normed1 = (layer_norm(flat) * (1.0 + spread_out(scale1)) + spread_out(shift1)).astype(
        jnp.bfloat16
    )
    local_width = qkv_w.shape[2]
    heads_local = local_width // HD
    qkv = jnp.dot(
        normed1.reshape(batch * per_image, width),
        qkv_w.reshape(width, 3 * local_width),
        preferred_element_type=jnp.float32,
    )
    qkv = qkv.astype(jnp.bfloat16).reshape(batch, per_image, 3, heads_local, HD)
    query = qkv[:, :, 0]
    key_local = qkv[:, :, 1]
    value_local = qkv[:, :, 2]
    scale = 1.0 / math.sqrt(HD)
    fresh = (
        jnp.einsum("bqhd,bkhd->bhqk", query, key_local, preferred_element_type=jnp.float32) * scale
    )
    top_start = jnp.max(fresh, axis=-1)
    probs = jnp.exp(fresh - top_start[..., None])
    mass_start = jnp.sum(probs, axis=-1)
    acc_start = jnp.einsum(
        "bhqk,bkhd->bhqd",
        probs.astype(jnp.bfloat16),
        value_local,
        preferred_element_type=jnp.float32,
    )
    stale_local = stale_kv.reshape(2, batch, -1, local_width)
    per_device = stale_local.shape[2]
    piece = lax.all_gather(stale_local, "row", axis=2, tiled=True)
    key_count = piece.shape[2]
    coarse_key = piece[0].reshape(batch, key_count, heads_local, HD)
    coarse_value = piece[1].reshape(batch, key_count, heads_local, HD)
    scores = jnp.einsum(
        "bqhd,bkhd->bhqk", query, coarse_key, preferred_element_type=jnp.float32
    ) * scale + math.log(4.0)
    key_device = jnp.arange(key_count, dtype=jnp.int32) // per_device
    scores = jnp.where((key_device == row_index)[None, None, None, :], jnp.float32(-1e30), scores)
    new_top = jnp.maximum(top_start, jnp.max(scores, axis=-1))
    shrink = jnp.exp(top_start - new_top)
    weights = jnp.exp(scores - new_top[..., None])
    new_mass = mass_start * shrink + jnp.sum(weights, axis=-1)
    new_acc = acc_start * shrink[..., None] + jnp.einsum(
        "bhqk,bkhd->bhqd",
        weights.astype(jnp.bfloat16),
        coarse_value,
        preferred_element_type=jnp.float32,
    )
    attended = (new_acc / new_mass[..., None]).astype(jnp.bfloat16)
    attended = attended.transpose(0, 2, 1, 3).reshape(batch * per_image, local_width)
    attn_part = jnp.dot(attended, out_w, preferred_element_type=jnp.float32).reshape(
        batch, tile_rows, full_cols, width
    )
    half_cols = full_cols // head_count
    col_start = head_index * half_cols
    projected = lax.psum(attn_part.astype(jnp.bfloat16), "head").astype(jnp.float32)
    mid = (flat + spread_out(gate1) * projected).astype(jnp.bfloat16)
    normed2 = (
        layer_norm(mid.astype(jnp.float32)) * (1.0 + spread_out(scale2)) + spread_out(shift2)
    ).astype(jnp.bfloat16)
    mid_half = lax.dynamic_slice_in_dim(mid, col_start, half_cols, 2)
    normed2_rows = normed2.reshape(batch * per_image, width)
    up_piece = lax.all_gather(fc1_w, "col", axis=1, tiled=True)
    down_piece = lax.all_gather(fc2_w, "col", axis=1, tiled=True)
    hidden = jax.nn.gelu(
        jnp.dot(normed2_rows, up_piece, preferred_element_type=jnp.float32), approximate=True
    ).astype(jnp.bfloat16)
    mlp_part = lax.dot_general(
        hidden, down_piece, (((1,), (1,)), ((), ())), preferred_element_type=jnp.float32
    )
    mlp_term = lax.psum_scatter(
        mlp_part.reshape(batch, tile_rows, full_cols, width).astype(jnp.bfloat16),
        "head",
        scatter_dimension=2,
        tiled=True,
    ).astype(jnp.float32)
    tokens_out = (mid_half.astype(jnp.float32) + spread_out(gate2) * mlp_term).astype(jnp.bfloat16)
    return tokens_out


def solution(mesh):
    placed = (
        P("col", "row", "head", None),
        P("col", "row", None, None),
        P("col"),
        P("col"),
        P(None, "col", "row", None, "head"),
        P(),
        P(),
        P(None, "row"),
        P(None, "row"),
        P("row", None),
        P(None, None, "head"),
        P("head", None),
        P(None, ("col", "head")),
        P(None, ("col", "head")),
    )
    return jax.shard_map(
        body, mesh=mesh, in_specs=placed, out_specs=P("col", "row", "head", None), check_vma=False
    )
```

profile of v0, /device:TPU:0, one launch (start us, length us, event | category | flops | bytes accessed | tf_op | source)
XLA Modules:
  0.0 356.1 jit_solution(11685589510042785841)
XLA Ops:
  8.5 8.5 %all_gather.12 = f32[3,4,64,4]{3,1,0,2:T(4,128)S(1)} all-gather(f32[3,4,32,4]{3,1,0,2:T(4,128)S(1)} %copy.66), channel_id=1, replica_groups=mesh['row'=8,'col'=2,'head'=2] {'head'}, dimensions={2}, use_global_device_ids=true | all-gather | bytes 18432 | tf_op jit(solution)/shard_map/all_gather | solution.py:135
  21.2 2.3 copy.80
  26.6 33.9 %psum.30 = bf16[3,6912]{1,0:T(4,128)(2,1)S(1)} all-reduce(bf16[3,6912]{1,0:T(4,128)(2,1)S(1)} %convolution_convert_fusion), channel_id=1, replica_groups=mesh['row'=8,'col'=2,'head'=2] {'row'}, use_global_device_ids=true, to_apply=%region_9.10 | all-reduce | flops 20736 | bytes 82944 | tf_op jit(solution)/shard_map/psum | solution.py:163
  64.6 14.1 %all-reduce.1 = (f32[3,4]{1,0:T(4,128)S(1)}, f32[3,4]{1,0:T(4,128)S(1)}) all-reduce(f32[3,4]{1,0:T(4,128)S(1)} %reduce_sum.105, f32[3,4]{1,0:T(4,128)S(1)} %reduce_sum.102), channel_id=1, replica_groups=mesh['row'=8,'col'=2,'head'=2] {'row'}, use_global_device_ids=true, to_apply=%region_8.9 | all-reduce | flops 24 | bytes 192 | tf_op jit(solution)/shard_map/psum | solution.py:145
  78.8 4.5 %convert_reduce_fusion = (f32[3,4,64]{2,1,0:T(4,128)S(1)}, bf16[3,4,64,1152]{3,2,1,0:T(8,128)(2,1)S(1)}) fusion(f32[4,64,1152]{2,1,0:T(8,128)S(1)} %pad_maximum_fusion, f32[16,1152]{1,0:T(8,128)} %param.19, f32[3,4,64,16]{2,3,1,0:T(8,128)S(1)} %get-tuple-element.13, f32[3,16]{1,0:T(4,128)S(1)} %mul.254, f32[3,16]{1,0:T(4,128)S(1)} %sub.91), kind=kOutput, calls=%fused_computation.21 | convolution fusion | flops 173432064 | bytes 3075456 | tf_op jit(solution)/shard_map/bijf,fd->bijd/dot_general | solution.py:159
  85.3 5.0 %convolution_convert_fusion.2 = bf16[768,1728]{0,1:T(8,128)(2,1)} fusion(bf16[768,1152]{1,0:T(8,128)(2,1)S(1)} %bitcast.108, bf16[1152,1728]{0,1:T(8,128)(2,1)S(1)} %bitcast.112), kind=kOutput, calls=%fused_computation.44 | convolution fusion | flops 3058974720 | bytes 8404992 | tf_op jit(solution)/shard_map/dot_general | solution.py:174
  90.3 6.9 %reshape.150 = bf16[3,256,3,8,72]{1,0,4,3,2:T(4,128)(2,1)} reshape(bf16[768,1728]{0,1:T(8,128)(2,1)} %convolution_convert_fusion.2) | data formatting | bytes 5308416 | tf_op jit(solution)/shard_map/reshape | solution.py:179
  97.2 3.3 fusion.104
  102.7 2.3 fusion.35
  105.0 9.4 %fusion.103 = (bf16[1,3,512,576]{3,0,1,2:T(2,128)(2,1)}, bf16[1,3,512,576]{3,0,1,2:T(2,128)(2,1)}) fusion(bf16[2,3,512,576]{3,0,1,2:T(2,128)(2,1)} %all-gather.4.cloned.1.call-done), kind=kLoop, calls=%fused_computation.162 | loop fusion | bytes 7077888 | tf_op jit(solution)/shard_map/slice | solution.py:200
  114.5 8.5 %copy.81 = bf16[1,3,512,576]{2,3,1,0:T(8,128)(2,1)} copy(bf16[1,3,512,576]{3,0,1,2:T(2,128)(2,1)} %get-tuple-element.14) | data formatting | bytes 3538944 | tf_op jit(solution)/shard_map/slice | solution.py:200
  123.0 7.8 %fusion.2 = (f32[3,8,256]{2,1,0:T(8,128)S(1)}, f32[3,8,256,512]{3,2,1,0:T(8,128)}) fusion(pred[512]{0:T(512)(128)(4,1)S(1)} %fusion.73, bf16[3,512,8,72]{1,3,2,0:T(8,128)(2,1)} %bitcast.109, bf16[3,256,1,8,72]{1,0,4,3,2:T(4,128)(2,1)S(1)} %get-tuple-element.18), kind=kOutput, calls=%fused_computation.5 | convolution fusion | flops 465561600 | bytes 15262208 | tf_op jit(solution)/shard_map/bqhd,bkhd->bhqk/dot_general | solution.py:202
  130.8 8.5 %copy.82 = bf16[1,3,512,576]{2,3,1,0:T(8,128)(2,1)} copy(bf16[1,3,512,576]{3,0,1,2:T(2,128)(2,1)} %get-tuple-element.15) | data formatting | bytes 3538944 | tf_op jit(solution)/shard_map/slice | solution.py:201
  139.3 8.3 %fusion = f32[3,8,256]{2,1,0:T(8,128)S(1)} fusion(f32[3,8,256,512]{3,2,1,0:T(8,128)} %get-tuple-element.52, f32[3,8,256]{2,1,0:T(8,128)S(1)} %max.18, pred[512]{0:T(512)(128)(4,1)S(1)} %fusion.73), kind=kLoop, calls=%fused_computation.2 | loop fusion | flops 15722496 | bytes 12632576 | tf_op jit(solution)/shard_map/reduce_sum | solution.py:210
  147.6 6.1 %fusion.41 = bf16[3,256,8,72]{1,3,2,0:T(8,128)(2,1)} fusion(f32[3,8,256,72]{2,3,1,0:T(8,128)} %fusion.35, bf16[3,512,8,72]{1,3,2,0:T(8,128)(2,1)} %bitcast.106, f32[3,8,256,512]{3,2,1,0:T(8,128)S(1)} %copy-done.3, f32[3,8,256]{2,1,0:T(8,128)S(1)} %max.18, pred[512]{0:T(512)(128)(4,1)S(1)} %fusion.73, f32[3,256,8]{1,2,0:T(8,128)S(1)} %get-tuple-element.11, ...), kind=kOutput, calls=%fused_computation.51 | convolution fusion | flops 470482944 | bytes 17080832 | tf_op jit(solution)/shard_map/bhqk,bkhd->bhqd/dot_general | solution.py:211
  153.8 4.0 %reshape.155 = bf16[3,4,64,576]{2,1,3,0:T(4,128)(2,1)} reshape(bf16[3,256,8,72]{1,3,2,0:T(8,128)(2,1)} %fusion.41) | data formatting | bytes 1769472 | tf_op jit(solution)/shard_map/dot_general | solution.py:219
  157.8 4.5 %convolution_convert_fusion.1 = bf16[3,4,64,1152]{3,2,1,0:T(8,128)(2,1)} fusion(bf16[3,4,64,576]{2,1,3,0:T(4,128)(2,1)} %reshape.155, bf16[576,1152]{1,0:T(8,128)(2,1)S(1)} %copy-done.6), kind=kOutput, calls=%fused_computation.43 | convolution fusion | flops 1020100608 | bytes 3981312 | tf_op jit(solution)/shard_map/dot_general | solution.py:219
  163.8 52.8 %all-reduce.4.cloned.1.call-done = bf16[3,4,64,1152]{3,2,1,0:T(8,128)(2,1)} async-done(((bf16[3,4,64,1152]{3,2,1,0:T(8,128)(2,1)}), bf16[3,4,64,1152]{3,2,1,0:T(8,128)(2,1)}) %all-reduce.4.cloned.1.call-update) | async-done | bytes 1769488 | tf_op jit(solution)/shard_map/psum | solution.py:224
  220.0 2.5 fusion.27
  222.5 9.3 %all-gather.6.cloned.1.call-done = bf16[1152,2304]{1,0:T(8,128)(2,1)} async-done(((bf16[1152,1152]{1,0:T(8,128)(2,1)}), bf16[1152,2304]{1,0:T(8,128)(2,1)}) %all-gather.6.cloned.1.call-update) | async-done | bytes 5308432 | tf_op jit(solution)/shard_map/all_gather | solution.py:231
  231.8 70.6 %all-gather.8.cloned.1.call-done = bf16[1152,2304]{1,0:T(8,128)(2,1)} async-done(((bf16[1152,1152]{1,0:T(8,128)(2,1)}), bf16[1152,2304]{1,0:T(8,128)(2,1)}) %all-gather.8.cloned.1.call-update) | async-done | bytes 5308432 | tf_op jit(solution)/shard_map/all_gather | solution.py:232
  302.4 15.5 %fusion.31 = bf16[768,1152]{1,0:T(8,128)(2,1)} fusion(bf16[1152,2304]{1,0:T(8,128)(2,1)} %all-gather.8.cloned.1.call-done, bf16[768,1152]{1,0:T(8,128)(2,1)} %bitcast.107, bf16[1152,2304]{1,0:T(8,128)(2,1)} %all-gather.6.cloned.1.call-done), kind=kOutput, calls=%fused_computation.41 | convolution fusion | flops 8170536960 | bytes 14155776 | tf_op jit(solution)/shard_map/dot_general | solution.py:236
  317.9 28.5 %reduce-scatter.2.cloned.1.call-done = bf16[3,4,32,1152]{3,2,1,0:T(8,128)(2,1)} async-done(((bf16[3,4,64,1152]{3,2,1,0:T(8,128)(2,1)}), bf16[3,4,32,1152]{3,2,1,0:T(8,128)(2,1)}) %reduce-scatter.2.cloned.1.call-update) | async-done | bytes 884752 | tf_op jit(solution)/shard_map/reduce_scatter | solution.py:239
  346.4 2.6 add_convert_fusion
  (104 shorter events, 21.3 us)
Async XLA Ops:
  7.4 18.5 %copy-start = (bf16[144,6912]{1,0:T(8,128)(2,1)S(1)}, bf16[144,6912]{1,0:T(8,128)(2,1)}, u32[]{:S(2)}) copy-start(bf16[144,6912]{1,0:T(8,128)(2,1)} %param.23) | copy-start | bytes 5971972
  7.4 54.4 %copy-start.11 = (s32[3]{0:T(128)S(1)}, s32[3]{0:T(128)}, u32[]{:S(2)}) copy-start(s32[3]{0:T(128)} %param.16) | copy-start | bytes 40
  7.4 18.5 %copy-start.10 = (s32[3]{0:T(128)S(1)}, s32[3]{0:T(128)}, u32[]{:S(2)}) copy-start(s32[3]{0:T(128)} %param.17) | copy-start | bytes 40
  7.4 18.5 %copy-start.7 = (bf16[1001,144]{0,1:T(8,128)(2,1)S(1)}, bf16[1001,144]{0,1:T(8,128)(2,1)}, u32[]{:S(2)}) copy-start(bf16[1001,144]{0,1:T(8,128)(2,1)} %param.22) | copy-start | bytes 864868
  7.4 97.6 %all-gather.4.cloned.1.call-start = ((), (), s32[]{:S(2)}) async-start(), calls=%async_computation.1 | async-start | bytes 4423680 | tf_op jit(solution)/shard_map/all_gather | solution.py:198
  17.0 0.7 copy-start.4
  18.6 44.7 %collective-permute-start = (f32[3,1,64,4]{3,1,0,2:T(1,128)}, f32[3,1,64,4]{3,1,0,2:T(1,128)S(1)}, u32[]{:S(2)}, u32[]{:S(2)}) collective-permute-start(f32[3,1,64,4]{3,1,0,2:T(1,128)} %get-tuple-element.21), channel_id=1, source_target_pairs={{0,4},{4,8},{8,12},{12,16},{16,20},{20,24},{24,28},{1,5},{5,9},{9,... | collective-permute-start | bytes 9224 | tf_op jit(solution)/shard_map/ppermute | solution.py:16
  19.9 43.4 %collective-permute-start.1 = (f32[3,1,64,4]{3,1,0,2:T(1,128)}, f32[3,1,64,4]{3,1,0,2:T(1,128)S(1)}, u32[]{:S(2)}, u32[]{:S(2)}) collective-permute-start(f32[3,1,64,4]{3,1,0,2:T(1,128)} %get-tuple-element.22), channel_id=1, source_target_pairs={{4,0},{8,4},{12,8},{16,12},{20,16},{24,20},{28,24},{5,1},{9,5},{13... | collective-permute-start | bytes 9224 | tf_op jit(solution)/shard_map/ppermute | solution.py:19
  23.5 193.1 %all-reduce.4.cloned.1.call-start = ((), (), s32[]{:S(2)}) async-start(), calls=%async_computation.2 | async-start | bytes 3538944 | tf_op jit(solution)/shard_map/psum | solution.py:224
  26.6 36.4 %copy-start.5 = (f32[3,4,64,4]{3,1,0,2:T(4,128)S(1)}, f32[3,4,64,4]{3,1,0,2:T(4,128)}, u32[]{:S(2)}) copy-start(f32[3,4,64,4]{3,1,0,2:T(4,128)} %copy-done.4) | copy-start | bytes 36868
  61.5 2.7 copy-start.8
  78.8 6.5 %copy-start.12 = (bf16[1152,3,576]{0,2,1:T(8,128)(2,1)S(1)}, bf16[1152,3,576]{0,2,1:T(8,128)(2,1)}, u32[]{:S(2)}) copy-start(bf16[1152,3,576]{0,2,1:T(8,128)(2,1)} %param.24) | copy-start | bytes 11943940
  139.3 8.4 %copy-start.3 = (f32[3,8,256,512]{3,2,1,0:T(8,128)S(1)}, f32[3,8,256,512]{3,2,1,0:T(8,128)}, u32[]{:S(2)}) copy-start(f32[3,8,256,512]{3,2,1,0:T(8,128)} %get-tuple-element.52) | copy-start | bytes 37748740
  153.8 4.0 %copy-start.6 = (bf16[576,1152]{1,0:T(8,128)(2,1)S(1)}, bf16[576,1152]{1,0:T(8,128)(2,1)}, u32[]{:S(2)}) copy-start(bf16[576,1152]{1,0:T(8,128)(2,1)} %param.25) | copy-start | bytes 3981316
  162.3 54.3 %copy-start.9 = (f32[3,1152]{1,0:T(4,128)S(1)}, f32[3,1152]{1,0:T(4,128)}, u32[]{:S(2)}) copy-start(f32[3,1152]{1,0:T(4,128)} %get-tuple-element.27) | copy-start | bytes 41476
  162.3 69.5 %all-gather.6.cloned.1.call-start = ((), (), s32[]{:S(2)}) async-start(), calls=%async_computation.3 | async-start | bytes 7962624 | tf_op jit(solution)/shard_map/all_gather | solution.py:231
  162.9 139.5 %all-gather.8.cloned.1.call-start = ((), (), s32[]{:S(2)}) async-start(), calls=%async_computation.4 | async-start | bytes 7962624 | tf_op jit(solution)/shard_map/all_gather | solution.py:232
  163.5 182.9 %reduce-scatter.2.cloned.1.call-start = ((), (), s32[]{:S(2)}) async-start(), calls=%async_computation.5 | async-start | bytes 2654208 | tf_op jit(solution)/shard_map/reduce_scatter | solution.py:239
  218.8 1.2 copy-start.2
  302.4 46.6 %copy-start.1 = (bf16[144,6912]{1,0:T(8,128)(2,1)S(1)}, bf16[144,6912]{1,0:T(8,128)(2,1)}, u32[]{:S(2)}) copy-start(bf16[144,6912]{1,0:T(8,128)(2,1)} %param.23) | copy-start | bytes 5971972
Sparse Core Ops, SparseCore 0:
  23.6 50.2 all-gather.3
  162.4 54.0 all-reduce.3
  318.0 28.3 reduce-scatter.1
Sparse Core Ops, SparseCore 1:
  164.4 67.4 all-gather.5
  233.2 69.1 all-gather.7
where the time goes:
time: 357 us; the launch traced here: 356 us
  waiting for transfers between devices  162 us (45%)
  blocking collectives  56.5 us (16%)
  matrix products  49 us (14%)
  local copies, waits for them, and re-layouts  47.9 us (13%)
  other arithmetic  22.4 us (6%)
  between operations  14.9 us (4%)
    all_gather x1, waiting for transfers between devices, body(): down_piece = lax.all_gather(fc2_w, 'col', axis=1, tiled=True)  70.6 us
    psum x1, waiting for transfers between devices, body(): lax.psum(attn_part.astype(jnp.bfloat16), 'head').astype(jnp.float32)  52.8 us
    psum x1, blocking collectives, body(): lax.psum(jnp.dot(cond_act, ada_w, preferred_element_type=jnp.float32).ast...  33.9 us
    reduce_scatter x1, waiting for transfers between devices, body(): lax.psum_scatter(mlp_part.reshape(batch, tile_rows, full_cols, width).ast...  28.5 us
    slice x2, local copies, waits for them, and re-layouts, body(): coarse_key = piece[0].reshape(batch, key_count, heads_local, HD)  17.9 us
    dot_general x1, matrix products, body(): lax.dot_general(hidden, down_piece, (((1,), (1,)), ((), ())), preferred_e...  15.5 us
    psum x1, blocking collectives, body(): lax.psum((jnp.sum(grouped, axis=(1, 2, 3)), jnp.sum(grouped * grouped, ax...  14.1 us
    all_gather x1, waiting for transfers between devices, body(): up_piece = lax.all_gather(fc1_w, 'col', axis=1, tiled=True)  9.34 us
  transfers between devices with their start and end apart: 7, of which 4 were waited for; matrix products, arithmetic and copies ran while one was open for 11% of the time, Pallas kernels for 0%

commit v1 on v0

--- a/solution.py
+++ b/solution.py
@@ -6,6 +6,12 @@
 
 HD = 72
 TSTEPS = 1000
+
+
+def add_all(shard, axis):
+    blocks = lax.all_gather(shard, axis, axis=0, tiled=False)
+    summed = blocks.sum(axis=0)
+    return summed
 
 
 def padded_2(block, sides, width):
@@ -221,7 +227,7 @@
     )
     half_cols = full_cols // head_count
     col_start = head_index * half_cols
-    projected = lax.psum(attn_part.astype(jnp.bfloat16), "head").astype(jnp.float32)
+    projected = add_all(attn_part.astype(jnp.bfloat16), "head").astype(jnp.float32)
     mid = (flat + spread_out(gate1) * projected).astype(jnp.bfloat16)
     normed2 = (
         layer_norm(mid.astype(jnp.float32)) * (1.0 + spread_out(scale2)) + spread_out(shift2)

time: 357 us -> 405 us (1.13)
  waiting for transfers between devices: 162 us -> 207 us
  other arithmetic: 22.4 us -> 26.8 us
    all_gather x1, waiting for transfers between devices: 9.34 us -> 70.7 us  [body(): up_piece = lax.all_gather(fc1_w, 'col', axis=1, tiled=True)]
    psum x1 -> x0, waiting for transfers between devices: 52.8 us -> none  [body(): lax.psum(attn_part.astype(jnp.bfloat16), 'head').astype(jnp.float32)]
    all_gather x0 -> x1, waiting for transfers between devices: none -> 46.1 us  [add_all(): blocks = lax.all_gather(shard, axis, axis=0, tiled=False)]
    all_gather x1, waiting for transfers between devices: 70.6 us -> 60.6 us  [body(): down_piece = lax.all_gather(fc2_w, 'col', axis=1, tiled=True)]
    reduce_sum x0 -> x1, other arithmetic: none -> 4.35 us  [add_all(): summed = blocks.sum(axis=0)]
where the time goes in v1:
time: 405 us; the launch traced here: 404 us
  waiting for transfers between devices  207 us (51%)
  blocking collectives  56.5 us (14%)
  matrix products  48.9 us (12%)
  local copies, waits for them, and re-layouts  47.9 us (12%)
  other arithmetic  26.8 us (7%)
  between operations  13.5 us (3%)
    all_gather x1, waiting for transfers between devices, body(): up_piece = lax.all_gather(fc1_w, 'col', axis=1, tiled=True)  70.7 us
    all_gather x1, waiting for transfers between devices, body(): down_piece = lax.all_gather(fc2_w, 'col', axis=1, tiled=True)  60.6 us
    all_gather x1, waiting for transfers between devices, add_all(): blocks = lax.all_gather(shard, axis, axis=0, tiled=False)  46.1 us
    psum x1, blocking collectives, body(): lax.psum(jnp.dot(cond_act, ada_w, preferred_element_type=jnp.float32).ast...  33.9 us
    reduce_scatter x1, waiting for transfers between devices, body(): lax.psum_scatter(mlp_part.reshape(batch, tile_rows, full_cols, width).ast...  28.5 us
    slice x2, local copies, waits for them, and re-layouts, body(): coarse_key = piece[0].reshape(batch, key_count, heads_local, HD)  17.9 us
    dot_general x1, matrix products, body(): lax.dot_general(hidden, down_piece, (((1,), (1,)), ((), ())), preferred_e...  15.5 us
    psum x1, blocking collectives, body(): lax.psum((jnp.sum(grouped, axis=(1, 2, 3)), jnp.sum(grouped * grouped, ax...  14.1 us
  transfers between devices with their start and end apart: 7, of which 4 were waited for; matrix products, arithmetic and copies ran while one was open for 11% of the time, Pallas kernels for 0%

profile of v1, /device:TPU:0, one launch (start us, length us, event | category | flops | bytes accessed | tf_op | source)
XLA Modules:
  0.0 403.9 jit_solution(1836817710751549239)
XLA Ops:
  7.6 8.5 %all_gather.18 = f32[3,4,64,4]{3,1,0,2:T(4,128)S(1)} all-gather(f32[3,4,32,4]{3,1,0,2:T(4,128)S(1)} %copy.66), channel_id=1, replica_groups=mesh['row'=8,'col'=2,'head'=2] {'head'}, dimensions={2}, use_global_device_ids=true | all-gather | bytes 18432 | tf_op jit(solution)/shard_map/all_gather | solution.py:141
  25.8 33.9 %psum.23 = bf16[3,6912]{1,0:T(4,128)(2,1)S(1)} all-reduce(bf16[3,6912]{1,0:T(4,128)(2,1)S(1)} %convolution_convert_fusion), channel_id=1, replica_groups=mesh['row'=8,'col'=2,'head'=2] {'row'}, use_global_device_ids=true, to_apply=%region_9.10 | all-reduce | flops 20736 | bytes 82944 | tf_op jit(solution)/shard_map/psum | solution.py:169
  63.7 14.1 %all-reduce.1 = (f32[3,4]{1,0:T(4,128)S(1)}, f32[3,4]{1,0:T(4,128)S(1)}) all-reduce(f32[3,4]{1,0:T(4,128)S(1)} %reduce_sum.117, f32[3,4]{1,0:T(4,128)S(1)} %reduce_sum.114), channel_id=1, replica_groups=mesh['row'=8,'col'=2,'head'=2] {'row'}, use_global_device_ids=true, to_apply=%region_8.9 | all-reduce | flops 24 | bytes 192 | tf_op jit(solution)/shard_map/psum | solution.py:151
  78.0 4.5 %convert_reduce_fusion = (f32[3,4,64]{2,1,0:T(4,128)S(1)}, bf16[3,4,64,1152]{3,2,1,0:T(8,128)(2,1)S(1)}) fusion(f32[4,64,1152]{2,1,0:T(8,128)S(1)} %pad_maximum_fusion, f32[16,1152]{1,0:T(8,128)} %param.19, f32[3,4,64,16]{2,3,1,0:T(8,128)S(1)} %get-tuple-element.13, f32[3,16]{1,0:T(4,128)S(1)} %mul.254, f32[3,16]{1,0:T(4,128)S(1)} %sub.91), kind=kOutput, calls=%fused_computation.21 | convolution fusion | flops 173432064 | bytes 3075456 | tf_op jit(solution)/shard_map/bijf,fd->bijd/dot_general | solution.py:165
  84.5 5.0 %convolution_convert_fusion.2 = bf16[768,1728]{0,1:T(8,128)(2,1)} fusion(bf16[768,1152]{1,0:T(8,128)(2,1)S(1)} %bitcast.110, bf16[1152,1728]{0,1:T(8,128)(2,1)S(1)} %bitcast.114), kind=kOutput, calls=%fused_computation.44 | convolution fusion | flops 3058974720 | bytes 8404992 | tf_op jit(solution)/shard_map/dot_general | solution.py:180
  89.5 6.9 %reshape.150 = bf16[3,256,3,8,72]{1,0,4,3,2:T(4,128)(2,1)} reshape(bf16[768,1728]{0,1:T(8,128)(2,1)} %convolution_convert_fusion.2) | data formatting | bytes 5308416 | tf_op jit(solution)/shard_map/reshape | solution.py:185
  96.4 3.3 fusion.104
  101.8 2.3 fusion.35
  104.2 9.4 %fusion.103 = (bf16[1,3,512,576]{3,0,1,2:T(2,128)(2,1)}, bf16[1,3,512,576]{3,0,1,2:T(2,128)(2,1)}) fusion(bf16[2,3,512,576]{3,0,1,2:T(2,128)(2,1)} %all-gather.6.cloned.1.call-done), kind=kLoop, calls=%fused_computation.162 | loop fusion | bytes 7077888 | tf_op jit(solution)/shard_map/slice | solution.py:206
  113.6 8.5 %copy.81 = bf16[1,3,512,576]{2,3,1,0:T(8,128)(2,1)} copy(bf16[1,3,512,576]{3,0,1,2:T(2,128)(2,1)} %get-tuple-element.14) | data formatting | bytes 3538944 | tf_op jit(solution)/shard_map/slice | solution.py:206
  122.1 7.8 %fusion.2 = (f32[3,8,256]{2,1,0:T(8,128)S(1)}, f32[3,8,256,512]{3,2,1,0:T(8,128)}) fusion(pred[512]{0:T(512)(128)(4,1)S(1)} %fusion.73, bf16[3,512,8,72]{1,3,2,0:T(8,128)(2,1)} %bitcast.111, bf16[3,256,1,8,72]{1,0,4,3,2:T(4,128)(2,1)S(1)} %get-tuple-element.18), kind=kOutput, calls=%fused_computation.5 | convolution fusion | flops 465561600 | bytes 15262208 | tf_op jit(solution)/shard_map/bqhd,bkhd->bhqk/dot_general | solution.py:208
  129.9 8.5 %copy.82 = bf16[1,3,512,576]{2,3,1,0:T(8,128)(2,1)} copy(bf16[1,3,512,576]{3,0,1,2:T(2,128)(2,1)} %get-tuple-element.15) | data formatting | bytes 3538944 | tf_op jit(solution)/shard_map/slice | solution.py:207
  138.4 8.3 %fusion = f32[3,8,256]{2,1,0:T(8,128)S(1)} fusion(f32[3,8,256,512]{3,2,1,0:T(8,128)} %get-tuple-element.52, f32[3,8,256]{2,1,0:T(8,128)S(1)} %max.18, pred[512]{0:T(512)(128)(4,1)S(1)} %fusion.73), kind=kLoop, calls=%fused_computation.2 | loop fusion | flops 15722496 | bytes 12632576 | tf_op jit(solution)/shard_map/reduce_sum | solution.py:216
  146.8 6.1 %fusion.41 = bf16[3,256,8,72]{1,3,2,0:T(8,128)(2,1)} fusion(f32[3,8,256,72]{2,3,1,0:T(8,128)} %fusion.35, bf16[3,512,8,72]{1,3,2,0:T(8,128)(2,1)} %bitcast.108, f32[3,8,256,512]{3,2,1,0:T(8,128)S(1)} %copy-done.3, f32[3,8,256]{2,1,0:T(8,128)S(1)} %max.18, pred[512]{0:T(512)(128)(4,1)S(1)} %fusion.73, f32[3,256,8]{1,2,0:T(8,128)S(1)} %get-tuple-element.11, ...), kind=kOutput, calls=%fused_computation.51 | convolution fusion | flops 470482944 | bytes 17080832 | tf_op jit(solution)/shard_map/bhqk,bkhd->bhqd/dot_general | solution.py:217
  152.9 4.0 reshape.156
  156.9 4.4 %convolution_convert_fusion.1 = bf16[3,4,64,1152]{3,2,1,0:T(8,128)(2,1)} fusion(bf16[3,4,64,576]{2,1,3,0:T(4,128)(2,1)} %reshape.156, bf16[576,1152]{1,0:T(8,128)(2,1)S(1)} %copy-done.6), kind=kOutput, calls=%fused_computation.43 | convolution fusion | flops 1020100608 | bytes 3981312 | tf_op jit(solution)/shard_map/dot_general | solution.py:225
  163.0 46.1 %all-gather.12.cloned.1.call-done = bf16[6,4,64,1152]{3,2,1,0:T(8,128)(2,1)} async-done(((bf16[3,4,64,1152]{3,2,1,0:T(8,128)(2,1)}), bf16[6,4,64,1152]{3,2,1,0:T(8,128)(2,1)}) %all-gather.12.cloned.1.call-update) | async-done | bytes 3538960 | tf_op jit(solution)/shard_map/all_gather | solution.py:12
  209.1 4.3 %reduce_sum.124 = bf16[3,4,64,1152]{3,2,1,0:T(8,128)(2,1)} reduce(bf16[2,3,4,64,1152]{4,3,2,1,0:T(8,128)(2,1)} %bitcast.105, bf16[]{:T(256)} %constant.99.clone.1), dimensions={0}, to_apply=%region_16.17 | reduce | flops 884736 | bytes 5308418 | tf_op jit(solution)/shard_map/reduce_sum | solution.py:13
  216.9 2.5 fusion.27
  219.4 60.6 %all-gather.10.cloned.1.call-done = bf16[1152,2304]{1,0:T(8,128)(2,1)} async-done(((bf16[1152,1152]{1,0:T(8,128)(2,1)}), bf16[1152,2304]{1,0:T(8,128)(2,1)}) %all-gather.10.cloned.1.call-update) | async-done | bytes 5308432 | tf_op jit(solution)/shard_map/all_gather | solution.py:238
  280.0 70.7 %all-gather.8.cloned.1.call-done = bf16[1152,2304]{1,0:T(8,128)(2,1)} async-done(((bf16[1152,1152]{1,0:T(8,128)(2,1)}), bf16[1152,2304]{1,0:T(8,128)(2,1)}) %all-gather.8.cloned.1.call-update) | async-done | bytes 5308432 | tf_op jit(solution)/shard_map/all_gather | solution.py:237
  350.7 15.5 %fusion.31 = bf16[768,1152]{1,0:T(8,128)(2,1)} fusion(bf16[1152,2304]{1,0:T(8,128)(2,1)} %all-gather.10.cloned.1.call-done, bf16[768,1152]{1,0:T(8,128)(2,1)} %bitcast.109, bf16[1152,2304]{1,0:T(8,128)(2,1)} %all-gather.8.cloned.1.call-done), kind=kOutput, calls=%fused_computation.41 | convolution fusion | flops 8170536960 | bytes 14155776 | tf_op jit(solution)/shard_map/dot_general | solution.py:242
  366.3 28.5 %reduce-scatter.2.cloned.1.call-done = bf16[3,4,32,1152]{3,2,1,0:T(8,128)(2,1)} async-done(((bf16[3,4,64,1152]{3,2,1,0:T(8,128)(2,1)}), bf16[3,4,32,1152]{3,2,1,0:T(8,128)(2,1)}) %reduce-scatter.2.cloned.1.call-update) | async-done | bytes 884752 | tf_op jit(solution)/shard_map/reduce_scatter | solution.py:245
  394.7 2.6 add_convert_fusion
  (105 shorter events, 23.8 us)
Async XLA Ops:
  6.5 18.5 %copy-start = (bf16[144,6912]{1,0:T(8,128)(2,1)S(1)}, bf16[144,6912]{1,0:T(8,128)(2,1)}, u32[]{:S(2)}) copy-start(bf16[144,6912]{1,0:T(8,128)(2,1)} %param.23) | copy-start | bytes 5971972
  6.5 54.4 %copy-start.11 = (s32[3]{0:T(128)S(1)}, s32[3]{0:T(128)}, u32[]{:S(2)}) copy-start(s32[3]{0:T(128)} %param.16) | copy-start | bytes 40
  6.5 18.5 %copy-start.10 = (s32[3]{0:T(128)S(1)}, s32[3]{0:T(128)}, u32[]{:S(2)}) copy-start(s32[3]{0:T(128)} %param.17) | copy-start | bytes 40
  6.5 18.5 %copy-start.7 = (bf16[1001,144]{0,1:T(8,128)(2,1)S(1)}, bf16[1001,144]{0,1:T(8,128)(2,1)}, u32[]{:S(2)}) copy-start(bf16[1001,144]{0,1:T(8,128)(2,1)} %param.22) | copy-start | bytes 864868
  6.5 97.6 %all-gather.6.cloned.1.call-start = ((), (), s32[]{:S(2)}) async-start(), calls=%async_computation.1 | async-start | bytes 4423680 | tf_op jit(solution)/shard_map/all_gather | solution.py:204
  16.2 0.7 copy-start.4
  17.7 44.7 %collective-permute-start = (f32[3,1,64,4]{3,1,0,2:T(1,128)}, f32[3,1,64,4]{3,1,0,2:T(1,128)S(1)}, u32[]{:S(2)}, u32[]{:S(2)}) collective-permute-start(f32[3,1,64,4]{3,1,0,2:T(1,128)} %get-tuple-element.21), channel_id=1, source_target_pairs={{0,4},{4,8},{8,12},{12,16},{16,20},{20,24},{24,28},{1,5},{5,9},{9,... | collective-permute-start | bytes 9224 | tf_op jit(solution)/shard_map/ppermute | solution.py:22
  19.0 43.4 %collective-permute-start.1 = (f32[3,1,64,4]{3,1,0,2:T(1,128)}, f32[3,1,64,4]{3,1,0,2:T(1,128)S(1)}, u32[]{:S(2)}, u32[]{:S(2)}) collective-permute-start(f32[3,1,64,4]{3,1,0,2:T(1,128)} %get-tuple-element.22), channel_id=1, source_target_pairs={{4,0},{8,4},{12,8},{16,12},{20,16},{24,20},{28,24},{5,1},{9,5},{13... | collective-permute-start | bytes 9224 | tf_op jit(solution)/shard_map/ppermute | solution.py:25
  22.7 186.5 %all-gather.12.cloned.1.call-start = ((), (), s32[]{:S(2)}) async-start(), calls=%async_computation.5 | async-start | bytes 5308416 | tf_op jit(solution)/shard_map/all_gather | solution.py:12
  25.8 36.4 %copy-start.5 = (f32[3,4,64,4]{3,1,0,2:T(4,128)S(1)}, f32[3,4,64,4]{3,1,0,2:T(4,128)}, u32[]{:S(2)}) copy-start(f32[3,4,64,4]{3,1,0,2:T(4,128)} %copy-done.4) | copy-start | bytes 36868
  60.7 2.7 copy-start.8
  78.0 6.5 %copy-start.12 = (bf16[1152,3,576]{0,2,1:T(8,128)(2,1)S(1)}, bf16[1152,3,576]{0,2,1:T(8,128)(2,1)}, u32[]{:S(2)}) copy-start(bf16[1152,3,576]{0,2,1:T(8,128)(2,1)} %param.24) | copy-start | bytes 11943940
  138.4 8.4 %copy-start.3 = (f32[3,8,256,512]{3,2,1,0:T(8,128)S(1)}, f32[3,8,256,512]{3,2,1,0:T(8,128)}, u32[]{:S(2)}) copy-start(f32[3,8,256,512]{3,2,1,0:T(8,128)} %get-tuple-element.52) | copy-start | bytes 37748740
  152.9 4.0 copy-start.6
  161.4 118.6 %all-gather.10.cloned.1.call-start = ((), (), s32[]{:S(2)}) async-start(), calls=%async_computation.3 | async-start | bytes 7962624 | tf_op jit(solution)/shard_map/all_gather | solution.py:238
  162.1 51.3 %copy-start.9 = (f32[3,1152]{1,0:T(4,128)S(1)}, f32[3,1152]{1,0:T(4,128)}, u32[]{:S(2)}) copy-start(f32[3,1152]{1,0:T(4,128)} %get-tuple-element.27) | copy-start | bytes 41476
  162.2 188.6 %all-gather.8.cloned.1.call-start = ((), (), s32[]{:S(2)}) async-start(), calls=%async_computation.2 | async-start | bytes 7962624 | tf_op jit(solution)/shard_map/all_gather | solution.py:237
  162.7 232.0 %reduce-scatter.2.cloned.1.call-start = ((), (), s32[]{:S(2)}) async-start(), calls=%async_computation.4 | async-start | bytes 2654208 | tf_op jit(solution)/shard_map/reduce_scatter | solution.py:245
  215.7 1.2 copy-start.2
  350.7 46.6 %copy-start.1 = (bf16[144,6912]{1,0:T(8,128)(2,1)S(1)}, bf16[144,6912]{1,0:T(8,128)(2,1)}, u32[]{:S(2)}) copy-start(bf16[144,6912]{1,0:T(8,128)(2,1)} %param.23) | copy-start | bytes 5971972
Sparse Core Ops, SparseCore 0:
  22.8 50.2 all-gather.5
  161.5 47.5 all-gather.11
  210.7 69.2 all-gather.9
  281.4 69.2 all-gather.7
  366.4 28.3 reduce-scatter.1
